TPU v7x, 512 devices: a whole 4x8x8 slice. The times are simulated.
512 devices in a mesh: tok: 8 (over z), row: 8 (over y_hi, core), col: 8 (over x, y_lo).
Axes of the slice: x: 4, y: 8 (y_hi: 4, y_lo: 2; y = y_hi * 2 + y_lo), z: 8, core: 2. Of those that a mesh axis runs over, the one named last changes fastest.
Arguments:
- activations: bfloat16 [2048, 8192], P('tok', 'row'), may hold values from -8 to 8
- gradients: bfloat16 [2048, 8192], P('tok', 'col'), may hold values from -8 to 8
- act_basis: bfloat16 [8192, 8192], P('row', ('tok', 'col')), may hold values from -1 to 1
- grad_basis: bfloat16 [8192, 8192], P('col', 'row'), may hold values from -1 to 1
- eigen_noise: float32 [8192, 8192], P('row', ('tok', 'col')), may hold values from -6 to 6
Outputs:
- scales: float32 [8192, 8192], P('row', ('tok', 'col'))
- output_shift: bfloat16 [2048, 8192], P('tok', 'col')
All inputs are finite; a program needn't handle non-finite values.
Results may differ from a plain program's by a relative error of at most 0.0064.
Values may be sent and summed in bfloat16 or wider, within the bound.
No kernel may reach another device: no remote copies, remote signals or barrier semaphores. Data moves between devices by JAX's collectives and lax.ppermute only.
A program may use at most 64 MiB of HBM per device.

v0:
```python
import jax
import jax.numpy as jnp
from jax import lax
from jax.sharding import PartitionSpec as P

damping = 0.1


def contract(former, latter, former_dim, latter_dim):
    return lax.dot_general(
        former,
        latter,
        (((former_dim,), (latter_dim,)), ((), ())),
        preferred_element_type=jnp.float32,
    )


def over_rows(summands):
    return lax.psum(summands, "row")


def over_cols(summands):
    return lax.psum(summands, "col")


def shards(activations, gradients, act_basis, grad_basis, eigen_noise):
    token_count = activations.shape[0] * lax.axis_size("tok")
    basis_cols = lax.all_gather(act_basis, "tok", axis=1, tiled=True)
    act_proj = over_rows(contract(activations, basis_cols, 1, 0))
    grad_proj = over_cols(contract(gradients, grad_basis, 1, 0))
    act_sq = (act_proj * act_proj).astype(jnp.bfloat16)
    grad_sq = (grad_proj * grad_proj).astype(jnp.bfloat16)
    summed = lax.psum_scatter(
        contract(grad_sq, act_sq, 0, 0), "tok", scatter_dimension=1, tiled=True
    )
    scales = summed / token_count
    scaled = (eigen_noise * lax.rsqrt(token_count * (scales + damping))).astype(jnp.bfloat16)
    widened = lax.all_gather(scaled, "tok", axis=1, tiled=True)
    act_half = act_proj.astype(jnp.bfloat16)
    hidden = over_cols(contract(act_half, widened, 1, 1)).astype(jnp.bfloat16)
    output_shift = over_rows(contract(hidden, grad_basis, 1, 1)).astype(jnp.bfloat16)
    return (scales, output_shift)


def solution(mesh):
    in_specs = (
        P("tok", "row"),
        P("tok", "col"),
        P("row", ("tok", "col")),
        P("col", "row"),
        P("row", ("tok", "col")),
    )
    out_specs = (P("row", ("tok", "col")), P("tok", "col"))
    return jax.shard_map(shards, mesh=mesh, in_specs=in_specs, out_specs=out_specs, check_vma=False)
```

profile of v0, /device:TPU:17, one launch (start us, length us, event | category | flops | bytes accessed | tf_op | source)
XLA Modules:
  0.0 457.0 jit_solution(1851305855588722828)
XLA Ops:
  8.0 0.0 copy-start
  8.0 0.0 all-gather.3.cloned.1.call-start
  8.1 0.7 all-gather.3.cloned.1.call-update
  8.7 0.0 copy-start.1
  8.8 0.0 all-reduce.5.cloned.1.call-start
  8.8 0.8 copy-done
  9.6 2.7 fusion.5
  12.3 0.0 all-reduce.5.cloned.1.call-update
  12.4 0.0 all-reduce.7.cloned.1.call-start
  12.4 49.3 %all-gather.3.cloned.1.call-done = bf16[1024,1024]{1,0:T(8,128)(2,1)} async-done(((bf16[1024,128]{1,0:T(8,128)(2,1)}), bf16[1024,1024]{1,0:T(8,128)(2,1)}) %all-gather.3.cloned.1.call-update) | async-done | bytes 2097168 | tf_op jit(solution)/shard_map/all_gather | solution.py:28
  61.7 0.0 copy-done.1
  61.7 3.3 fusion.6
  65.0 0.0 all-reduce.7.cloned.1.call-update
  65.0 0.0 reduce-scatter.2.cloned.1.call-start
  65.0 38.5 %all-reduce.5.cloned.1.call-done = f32[256,1024]{1,0:T(8,128)} async-done(((f32[256,1024]{1,0:T(8,128)}), f32[256,1024]{1,0:T(8,128)}) %all-reduce.5.cloned.1.call-update) | async-done | bytes 1048592 | tf_op jit(solution)/shard_map/psum | solution.py:23
  103.5 89.2 %all-reduce.7.cloned.1.call-done = f32[256,1024]{1,0:T(8,128)} async-done(((f32[256,1024]{1,0:T(8,128)}), f32[256,1024]{1,0:T(8,128)}) %all-reduce.7.cloned.1.call-update) | async-done | bytes 1048592 | tf_op jit(solution)/shard_map/psum | solution.py:19
  192.7 4.2 fusion
  196.9 0.0 copy-start.2
  196.9 0.0 reduce-scatter.2.cloned.1.call-update
  196.9 0.0 all-gather.5.cloned.1.call-start
  197.0 57.3 %reduce-scatter.2.cloned.1.call-done = f32[1024,128]{1,0:T(8,128)} async-done(((f32[1024,1024]{1,0:T(8,128)}), f32[1024,128]{1,0:T(8,128)}) %reduce-scatter.2.cloned.1.call-update) | async-done | bytes 524304 | tf_op jit(solution)/shard_map/reduce_scatter | solution.py:33
  254.3 0.0 copy-done.2
  254.3 2.0 multiply_convert_fusion.4
  256.3 0.0 all-gather.5.cloned.1.call-update
  256.3 44.6 %all-gather.5.cloned.1.call-done = bf16[1024,1024]{1,0:T(8,128)(2,1)} async-done(((bf16[1024,128]{1,0:T(8,128)(2,1)}), bf16[1024,1024]{1,0:T(8,128)(2,1)}) %all-gather.5.cloned.1.call-update) | async-done | bytes 2097168 | tf_op jit(solution)/shard_map/all_gather | solution.py:38
  300.9 2.7 fusion.3
  303.6 64.5 %all-reduce.8 = bf16[256,1024]{1,0:T(8,128)(2,1)} all-reduce(f32[256,1024]{1,0:T(8,128)S(1)} %fusion.3), channel_id=1, replica_groups=mesh['tok'=8,'row'=8,'col'=8] {'col'}, use_global_device_ids=true, to_apply=%region_3.0 | all-reduce | flops 262144 | bytes 1572864 | tf_op jit(solution)/shard_map/psum | solution.py:23
  368.1 1.8 fusion.7
  369.8 80.0 %all-reduce.9 = bf16[256,1024]{1,0:T(8,128)(2,1)} all-reduce(f32[256,1024]{1,0:T(8,128)S(1)} %fusion.7), channel_id=1, replica_groups=mesh['tok'=8,'row'=8,'col'=8] {'row'}, use_global_device_ids=true, to_apply=%region_4.0 | all-reduce | flops 262144 | bytes 1572864 | tf_op jit(solution)/shard_map/psum | solution.py:19
Async XLA Ops:
  8.0 1.6 copy-start
  8.0 53.7 %all-gather.3.cloned.1.call-start = ((), (), s32[]{:S(2)}) async-start(), calls=%async_computation.2 | async-start | bytes 2359296 | tf_op jit(solution)/shard_map/all_gather | solution.py:28
  8.7 52.9 %copy-start.1 = (bf16[256,1024]{1,0:T(8,128)(2,1)S(1)}, bf16[256,1024]{1,0:T(8,128)(2,1)}, u32[]{:S(2)}) copy-start(bf16[256,1024]{1,0:T(8,128)(2,1)} %param.5) | copy-start | bytes 1572868
  8.8 94.8 %all-reduce.5.cloned.1.call-start = ((), (), s32[]{:S(2)}) async-start(), calls=%async_computation.1 | async-start | bytes 2097152 | tf_op jit(solution)/shard_map/psum | solution.py:23
  12.4 180.3 %all-reduce.7.cloned.1.call-start = ((), (), s32[]{:S(2)}) async-start(), calls=%async_computation.3 | async-start | bytes 2097152 | tf_op jit(solution)/shard_map/psum | solution.py:19
  65.0 189.3 %reduce-scatter.2.cloned.1.call-start = ((), (), s32[]{:S(2)}) async-start(), calls=%async_computation.4 | async-start | bytes 4718592 | tf_op jit(solution)/shard_map/reduce_scatter | solution.py:33
  196.9 57.4 %copy-start.2 = (f32[1024,128]{1,0:T(8,128)S(1)}, f32[1024,128]{1,0:T(8,128)}, u32[]{:S(2)}) copy-start(f32[1024,128]{1,0:T(8,128)} %param.9) | copy-start | bytes 1572868
  196.9 104.0 %all-gather.5.cloned.1.call-start = ((), (), s32[]{:S(2)}) async-start(), calls=%async_computation.5 | async-start | bytes 2359296 | tf_op jit(solution)/shard_map/all_gather | solution.py:38
Sparse Core Ops, SparseCore 0:
  10.8 50.8 all-gather.2
  197.1 57.1 reduce-scatter.1
  256.9 44.0 all-gather.4
Sparse Core Ops, SparseCore 1:
  12.4 91.0 all-reduce.4
  106.3 86.3 all-reduce.6
where the time goes:
time: 457 us
  waiting for transfers between devices  280 us (61%)
  blocking collectives  145 us (32%)
  between operations  15.2 us (3%)
  matrix products  14.7 us (3%)
    psum x1, waiting for transfers between devices, over_rows(): return lax.psum(summands, 'row')  89.2 us
    psum x1, blocking collectives, over_rows(): return lax.psum(summands, 'row')  80 us
    psum x1, blocking collectives, over_cols(): return lax.psum(summands, 'col')  64.5 us
    reduce_scatter x1, waiting for transfers between devices, shards(): lax.psum_scatter(contract(grad_sq, act_sq, 0, 0), 'tok', scatter_dimensio...  57.3 us
    all_gather x1, waiting for transfers between devices, shards(): basis_cols = lax.all_gather(act_basis, 'tok', axis=1, tiled=True)  49.3 us
    all_gather x1, waiting for transfers between devices, shards(): widened = lax.all_gather(scaled, 'tok', axis=1, tiled=True)  44.6 us
    psum x1, waiting for transfers between devices, over_cols(): return lax.psum(summands, 'col')  38.5 us
    dot_general x5, matrix products, contract(): lax.dot_general(former, latter, (((former_dim,), (latter_dim,)), ((), ())...  14.7 us
  transfers between devices with their start and end apart: 5, of which 5 were waited for; matrix products, arithmetic and copies ran while one was open for 1% of the time, Pallas kernels for 0%

commit v1 on v0

--- a/solution.py
+++ b/solution.py
@@ -20,7 +20,7 @@
 
 
 def over_cols(summands):
-    return lax.psum(summands, "col")
+    return jnp.sum(lax.all_gather(summands, "col"), axis=0)
 
 
 def shards(activations, gradients, act_basis, grad_basis, eigen_noise):

time: 457 us -> 693 us (1.52)
  the two profiles are of different devices: /device:TPU:17 before, /device:TPU:25 now
where the time goes in v1:
time: 693 us; the launch traced here: 692 us
  waiting for transfers between devices  586 us (85%)
  blocking collectives  64.4 us (9%)
  matrix products  15.1 us (2%)
  between operations  14.1 us (2%)
  other arithmetic  11.8 us (2%)
    all_gather x2, waiting for transfers between devices, over_cols(): return jnp.sum(lax.all_gather(summands, 'col'), axis=0)  352 us
    psum x1, waiting for transfers between devices, over_rows(): return lax.psum(summands, 'row')  82.2 us
    psum x1, blocking collectives, over_rows(): return lax.psum(summands, 'row')  64.4 us
    reduce_scatter x1, waiting for transfers between devices, shards(): lax.psum_scatter(contract(grad_sq, act_sq, 0, 0), 'tok', scatter_dimensio...  58 us
    all_gather x1, waiting for transfers between devices, shards(): basis_cols = lax.all_gather(act_basis, 'tok', axis=1, tiled=True)  48.7 us
    all_gather x1, waiting for transfers between devices, shards(): widened = lax.all_gather(scaled, 'tok', axis=1, tiled=True)  44.3 us
    dot_general x5, matrix products, contract(): lax.dot_general(former, latter, (((former_dim,), (latter_dim,)), ((), ())...  15.1 us
  transfers between devices with their start and end apart: 6, of which 6 were waited for; matrix products, arithmetic and copies ran while one was open for 2% of the time, Pallas kernels for 0%

profile of v1, /device:TPU:25, one launch (start us, length us, event | category | flops | bytes accessed | tf_op | source)
XLA Modules:
  0.0 692.5 jit_solution(17158341057360950852)
XLA Ops:
  7.2 0.0 copy-start
  7.2 0.0 all-gather.7.cloned.1.call-start
  7.2 0.7 all-gather.7.cloned.1.call-update
  7.9 0.0 copy-start.2
  7.9 0.0 all-gather.11.cloned.1.call-start
  8.0 0.8 copy-done
  8.8 2.7 fusion.5
  11.5 0.0 all-gather.11.cloned.1.call-update
  11.5 0.0 all-reduce.3.cloned.1.call-start
  11.6 48.7 %all-gather.7.cloned.1.call-done = bf16[1024,1024]{1,0:T(8,128)(2,1)} async-done(((bf16[1024,128]{1,0:T(8,128)(2,1)}), bf16[1024,1024]{1,0:T(8,128)(2,1)}) %all-gather.7.cloned.1.call-update) | async-done | bytes 2097168 | tf_op jit(solution)/shard_map/all_gather | solution.py:28
  60.3 0.0 copy-done.2
  60.3 3.3 fusion.6
  63.6 0.0 all-reduce.3.cloned.1.call-update
  63.6 0.0 reduce-scatter.2.cloned.1.call-start
  63.7 175.3 %all-gather.11.cloned.1.call-done = f32[2048,1024]{1,0:T(8,128)} async-done(((f32[256,1024]{1,0:T(8,128)}), f32[2048,1024]{1,0:T(8,128)}) %all-gather.11.cloned.1.call-update) | async-done | bytes 8388624 | tf_op jit(solution)/shard_map/all_gather | solution.py:23
  239.0 4.4 reduce_sum.18
  243.4 82.2 %all-reduce.3.cloned.1.call-done = f32[256,1024]{1,0:T(8,128)} async-done(((f32[256,1024]{1,0:T(8,128)}), f32[256,1024]{1,0:T(8,128)}) %all-reduce.3.cloned.1.call-update) | async-done | bytes 1048592 | tf_op jit(solution)/shard_map/psum | solution.py:19
  325.6 3.9 fusion
  329.5 0.0 reduce-scatter.2.cloned.1.call-update
  329.5 0.0 copy-start.1
  329.5 0.0 all-gather.9.cloned.1.call-start
  329.6 58.0 %reduce-scatter.2.cloned.1.call-done = f32[1024,128]{1,0:T(8,128)} async-done(((f32[1024,1024]{1,0:T(8,128)}), f32[1024,128]{1,0:T(8,128)}) %reduce-scatter.2.cloned.1.call-update) | async-done | bytes 524304 | tf_op jit(solution)/shard_map/reduce_scatter | solution.py:33
  387.6 2.2 multiply_convert_fusion.4
  389.7 0.0 all-gather.9.cloned.1.call-update
  389.8 0.0 all-gather.13.cloned.1.call-start
  389.8 44.3 %all-gather.9.cloned.1.call-done = bf16[1024,1024]{1,0:T(8,128)(2,1)} async-done(((bf16[1024,128]{1,0:T(8,128)(2,1)}), bf16[1024,1024]{1,0:T(8,128)(2,1)}) %all-gather.9.cloned.1.call-update) | async-done | bytes 2097168 | tf_op jit(solution)/shard_map/all_gather | solution.py:38
  434.1 0.0 copy-done.1
  434.1 3.4 fusion.3
  437.5 0.0 all-gather.13.cloned.1.call-update
  437.5 176.7 %all-gather.13.cloned.1.call-done = f32[2048,1024]{1,0:T(8,128)} async-done(((f32[256,1024]{1,0:T(8,128)}), f32[2048,1024]{1,0:T(8,128)}) %all-gather.13.cloned.1.call-update) | async-done | bytes 8388624 | tf_op jit(solution)/shard_map/all_gather | solution.py:23
  614.2 5.2 reduce_sum.19
  619.4 1.8 fusion.7
  621.2 64.4 %all-reduce.4 = bf16[256,1024]{1,0:T(8,128)(2,1)} all-reduce(f32[256,1024]{1,0:T(8,128)S(1)} %fusion.7), channel_id=1, replica_groups=mesh['tok'=8,'row'=8,'col'=8] {'row'}, use_global_device_ids=true, to_apply=%region_4.0 | all-reduce | flops 262144 | bytes 1572864 | tf_op jit(solution)/shard_map/psum | solution.py:19
Async XLA Ops:
  7.2 1.6 copy-start
  7.2 53.1 %all-gather.7.cloned.1.call-start = ((), (), s32[]{:S(2)}) async-start(), calls=%async_computation.1 | async-start | bytes 2359296 | tf_op jit(solution)/shard_map/all_gather | solution.py:28
  7.9 52.4 %copy-start.2 = (bf16[256,1024]{1,0:T(8,128)(2,1)S(1)}, bf16[256,1024]{1,0:T(8,128)(2,1)}, u32[]{:S(2)}) copy-start(bf16[256,1024]{1,0:T(8,128)(2,1)} %param.5) | copy-start | bytes 1572868
  7.9 231.1 %all-gather.11.cloned.1.call-start = ((), (), s32[]{:S(2)}) async-start(), calls=%async_computation.5 | async-start | bytes 9437184 | tf_op jit(solution)/shard_map/all_gather | solution.py:23
  11.5 314.0 %all-reduce.3.cloned.1.call-start = ((), (), s32[]{:S(2)}) async-start(), calls=%async_computation.2 | async-start | bytes 2097152 | tf_op jit(solution)/shard_map/psum | solution.py:19
  63.6 323.9 %reduce-scatter.2.cloned.1.call-start = ((), (), s32[]{:S(2)}) async-start(), calls=%async_computation.3 | async-start | bytes 4718592 | tf_op jit(solution)/shard_map/reduce_scatter | solution.py:33
  329.5 104.6 %copy-start.1 = (f32[256,1024]{1,0:T(8,128)S(1)}, f32[256,1024]{1,0:T(8,128)}, u32[]{:S(2)}) copy-start(f32[256,1024]{1,0:T(8,128)} %all-reduce.3.cloned.1.call-done) | copy-start | bytes 3145732
  329.5 104.6 %all-gather.9.cloned.1.call-start = ((), (), s32[]{:S(2)}) async-start(), calls=%async_computation.4 | async-start | bytes 2359296 | tf_op jit(solution)/shard_map/all_gather | solution.py:38
  389.8 224.5 %all-gather.13.cloned.1.call-start = ((), (), s32[]{:S(2)}) async-start(), calls=%async_computation.6 | async-start | bytes 9437184 | tf_op jit(solution)/shard_map/all_gather | solution.py:23
Sparse Core Ops, SparseCore 0:
  10.0 50.2 all-gather.6
  62.4 176.5 all-gather.10
  241.9 83.5 all-reduce.2
  329.6 57.9 reduce-scatter.1
  390.0 44.0 all-gather.8
  437.6 176.5 all-gather.12
